TPU v7x, 32 devices: a whole 2x2x4 slice. The times are simulated.
32 devices in a mesh: req: 16 (over z, y, core), tp: 2 (over x).
Axes of the slice: x: 2, y: 2, z: 4, core: 2. Of those that a mesh axis runs over, the one named last changes fastest.
Arguments:
- attn_ctx: bfloat16 [1024, 4096], P('req', 'tp'), may hold values from -6 to 6
- o_weight: bfloat16 [4096, 2880], P('tp'), may hold values from -0.09375 to 0.09375
- o_bias: bfloat16 [2880], replicated, may hold values from -3 to 3
- residual: bfloat16 [1024, 2880], P(('req', 'tp')), may hold values from -6 to 6
- post_gain: bfloat16 [2880], replicated, may hold values from 0.5 to 1.5
- router_weight: bfloat16 [2880, 8], replicated, may hold values from -0.01953125 to 0.01953125
- router_bias: float32 [8], replicated, may hold values from -0.4 to 0.4
- routes: int32 [1024, 4], P('req'), may hold values from 0 to 7, all different within a row; in each aligned block of 32 rows (0 to 31, 32 to 63, ...) at most 32 rows name the same one
- gate_up_weight: bfloat16 [16, 2880, 2, 1440], P('req', None, None, 'tp'), may hold values from -0.25 to 0.25
- gate_up_bias: bfloat16 [16, 2, 1440], P('req', None, 'tp'), may hold values from -3 to 3
- down_weight: bfloat16 [16, 1440, 2880], P('req', 'tp'), may hold values from -0.0546875 to 0.0546875
- down_bias: bfloat16 [8, 2880], replicated, may hold values from -3 to 3
- next_gain: bfloat16 [2880], replicated, may hold values from 0.5 to 1.5
Outputs:
- hidden_state: bfloat16 [1024, 2880], P(('req', 'tp'))
- normed_out: bfloat16 [1024, 2880], P(('req', 'tp'))
Inputs may be any that keep to these rules, and one draw needn't show every extreme that they name: `routes`: each row names 4 different experts. In each aligned block of 32 rows no expert is named by more than 32 rows, a bound that some block reaches.
All inputs are finite; a program needn't handle non-finite values.
Results may differ from a plain program's by a relative error of at most 0.017.
Values may be sent and summed in bfloat16 or wider, within the bound.
A program may use at most 128 MiB of HBM per device.

v0:
```python
import jax
import jax.numpy as jnp
from jax import lax
from jax.sharding import PartitionSpec as P


def rms_norm(values, gain):
    scale = lax.rsqrt(jnp.mean(values * values, axis=-1, keepdims=True) + 1e-05)
    return values * scale * gain.astype(jnp.float32)


def route_rows(state, route_ids, post_gain, router_weight, router_bias, experts):
    normed = rms_norm(state.astype(jnp.float32), post_gain).astype(jnp.bfloat16)
    logits = jnp.dot(normed, router_weight, preferred_element_type=jnp.float32) + router_bias
    onehot = (route_ids[:, :, None] == jnp.arange(experts, dtype=jnp.int32)[None, None, :]).astype(
        jnp.float32
    )
    picked = jnp.sum(onehot * logits[:, None, :], axis=2)
    expo = jnp.exp(picked)
    weights = expo / jnp.sum(expo, axis=1, keepdims=True)
    table = jnp.sum(onehot * weights[:, :, None], axis=1)
    return (normed, weights, table)


def slot_numbers(route_blocks, experts, capacity):
    onehot = (
        route_blocks[:, :, None] == jnp.arange(experts, dtype=jnp.int32)[None, None, :]
    ).astype(jnp.int32)
    ranks = jnp.cumsum(onehot, axis=1) - onehot
    slots = jnp.sum(ranks * onehot, axis=2)
    offsets = jnp.arange(route_blocks.shape[0], dtype=jnp.int32)[:, None] * capacity
    return slots + offsets


def place_rows(normed, targets, block, req_count, top_count):
    width = normed.shape[1]
    source = jnp.repeat(normed, top_count, axis=0)
    buffer = jnp.zeros((req_count * block, width), jnp.bfloat16)
    index = jnp.concatenate([targets, targets + block])
    buffer = buffer.at[index].set(jnp.concatenate([source, source], axis=0))
    return buffer.reshape(req_count, block, width)


def weigh_parts(flat, targets, block, weights, top_count):
    first = jnp.take(flat, targets, axis=0).astype(jnp.float32)
    second = jnp.take(flat, targets + block, axis=0).astype(jnp.float32)
    values = (first + second) * weights.reshape(-1)[:, None]
    return jnp.sum(values.reshape(-1, top_count, flat.shape[1]), axis=1)


def expert_apply(rows, gate_up_weight, gate_up_bias, down_weight):
    local_width = gate_up_weight.shape[3]
    weight_mat = gate_up_weight[0].reshape(gate_up_weight.shape[1], 2 * local_width)
    projected = jnp.dot(rows, weight_mat, preferred_element_type=jnp.float32)
    projected = projected + gate_up_bias[0].reshape(2 * local_width).astype(jnp.float32)
    gate = jnp.minimum(projected[:, :local_width], 7.0)
    upper = jnp.clip(projected[:, local_width:], -7.0, 7.0)
    act = ((upper + 1.0) * gate * jax.nn.sigmoid(1.702 * gate)).astype(jnp.bfloat16)
    return jnp.dot(act, down_weight[0], preferred_element_type=jnp.float32)


def per_device(
    attn_ctx,
    o_weight,
    o_bias,
    residual,
    post_gain,
    router_weight,
    router_bias,
    routes,
    gate_up_weight,
    gate_up_bias,
    down_weight,
    down_bias,
    next_gain,
):
    req_count = lax.axis_size("req")
    tp_count = lax.axis_size("tp")
    width = o_weight.shape[1]
    tokens_here = attn_ctx.shape[0]
    own_rows = tokens_here // tp_count
    experts = req_count // 2
    top_count = routes.shape[1]
    capacity = min(own_rows, max(2, 2 * top_count * own_rows // experts))
    own_start = lax.axis_index("tp") * own_rows
    bias_vec = o_bias.astype(jnp.float32)
    summed = lax.psum_scatter(
        jnp.dot(attn_ctx, o_weight, preferred_element_type=jnp.float32).astype(jnp.bfloat16),
        "tp",
        scatter_dimension=0,
        tiled=True,
    ).astype(jnp.float32)
    state = (residual.astype(jnp.float32) + summed + bias_vec).astype(jnp.bfloat16)
    own_routes = lax.dynamic_slice_in_dim(routes, own_start, own_rows, 0)
    normed, weights, table = route_rows(
        state, own_routes, post_gain, router_weight, router_bias, experts
    )
    slots = slot_numbers(own_routes.reshape(1, own_rows * top_count), experts, capacity)
    targets = 2 * own_routes.reshape(-1) * capacity + slots.reshape(-1)
    outgoing = place_rows(normed, targets, capacity, req_count, top_count)
    incoming = lax.all_to_all(outgoing, "req", split_axis=0, concat_axis=0, tiled=True)
    gathered = lax.all_gather(incoming[None], "tp", axis=0, tiled=True).reshape(-1, width)
    sums = lax.psum_scatter(
        expert_apply(gathered, gate_up_weight, gate_up_bias, down_weight).astype(jnp.bfloat16),
        "tp",
        scatter_dimension=0,
        tiled=True,
    ).astype(jnp.float32)
    returned = lax.all_to_all(
        sums.reshape(req_count, capacity, width).astype(jnp.bfloat16),
        "req",
        split_axis=0,
        concat_axis=0,
        tiled=True,
    ).astype(jnp.float32)
    mixed = weigh_parts(returned.reshape(-1, width), targets, capacity, weights, top_count)
    bias_terms = jnp.dot(table, down_bias.astype(jnp.float32), precision=lax.Precision.HIGHEST)
    hidden_state = (state.astype(jnp.float32) + mixed + bias_terms).astype(jnp.bfloat16)
    normed_out = rms_norm(hidden_state.astype(jnp.float32), next_gain).astype(jnp.bfloat16)
    return (hidden_state, normed_out)


def solution(mesh):
    return jax.shard_map(
        per_device,
        mesh=mesh,
        in_specs=(
            P("req", "tp"),
            P("tp", None),
            P(),
            P(("req", "tp"), None),
            P(),
            P(),
            P(),
            P("req", None),
            P("req", None, None, "tp"),
            P("req", None, "tp"),
            P("req", "tp", None),
            P(),
            P(),
        ),
        out_specs=(P(("req", "tp"), None), P(("req", "tp"), None)),
        check_vma=False,
    )
```

profile of v0, /device:TPU:13, one launch (start us, length us, event | category | flops | bytes accessed | tf_op | source)
XLA Modules:
  0.0 384.2 jit_solution(17498541128301382043)
XLA Ops:
  7.2 0.0 copy-start
  7.2 0.0 copy-start.9
  7.2 0.0 copy-start.5
  7.2 0.0 copy-start.6
  7.2 0.0 copy-start.3
  7.2 0.0 reduce-scatter.3.cloned.1.call-start
  7.3 0.9 copy-done
  8.1 8.7 %convolution_convert_fusion.1 = bf16[64,2880]{1,0:T(8,128)(2,1)} fusion(bf16[64,2048]{1,0:T(8,128)(2,1)S(1)} %copy-done, bf16[2048,2880]{0,1:T(8,128)(2,1)} %param.16), kind=kOutput, calls=%fused_computation.6 | convolution fusion | flops 755159040 | bytes 12427264 | tf_op jit(solution)/shard_map/dot_general | solution.py:88
  16.8 0.0 reduce-scatter.3.cloned.1.call-update
  16.9 0.0 all-gather.3.cloned.1.call-start
  16.9 0.0 copy-done.9
  16.9 0.1 constant_dynamic-slice_fusion
  17.0 0.1 copy.27
  17.1 0.1 reshape.264
  17.2 0.1 fusion.23
  17.3 0.0 copy-done.5
  17.3 0.0 copy-done.6
  17.3 0.2 reduce_window_sum.11
  17.5 0.2 select_reduce_fusion
  17.7 13.3 %reduce-scatter.3.cloned.1.call-done = bf16[32,2880]{1,0:T(8,128)(2,1)} async-done(((bf16[64,2880]{1,0:T(8,128)(2,1)}), bf16[32,2880]{1,0:T(8,128)(2,1)}) %reduce-scatter.3.cloned.1.call-update) | async-done | bytes 184336 | tf_op jit(solution)/shard_map/reduce_scatter | solution.py:87
  31.1 0.0 copy-done.3
  31.1 1.1 fusion.20
  32.2 0.1 fusion.22
  32.3 0.2 broadcast_in_dim.13
  32.5 1.2 reshape.265
  33.7 4.5 %scatter_custom_fusion = bf16[512,2880]{1,0:T(8,128)(2,1)S(1)} fusion(s32[256]{0:T(256)S(1)} %bitcast.25, bf16[128,2880]{1,0:T(8,128)(2,1)} %reshape.265, bf16[]{:T(256)} %constant.55, bf16[]{:T(256)} %constant.22.clone.1), kind=kCustom, calls=%fused_computation.16 | custom fusion | flops 2949120 | bytes 3686404 | tf_op jit(solution)/shard_map/scatter | solution.py:40
  38.3 73.3 %all_to_all.10 = bf16[16,32,2880]{2,1,0:T(8,128)(2,1)} all-to-all(bf16[16,32,2880]{2,1,0:T(8,128)(2,1)S(1)} %bitcast.23), channel_id=1, replica_groups=mesh['req'=16,'tp'=2] {'req'}, dimensions={0} | all-to-all | bytes 5898240 | tf_op jit(solution)/shard_map/all_to_all | solution.py:101
  111.5 0.0 copy-start.8
  111.5 0.0 slice-start
  111.5 0.0 all-gather.3.cloned.1.call-update
  111.6 0.2 reduce-scatter.5.cloned.1.call-start
  111.8 0.4 copy-done.8
  112.2 0.1 reshape.271
  112.3 75.7 %all-gather.3.cloned.1.call-done = bf16[32,32,2880]{2,1,0:T(8,128)(2,1)} async-done(((bf16[16,32,2880]{2,1,0:T(8,128)(2,1)}), bf16[32,32,2880]{2,1,0:T(8,128)(2,1)}) %all-gather.3.cloned.1.call-update) | async-done | bytes 5898256 | tf_op jit(solution)/shard_map/all_gather | solution.py:102
  188.0 0.0 slice-start.1
  188.0 13.7 %convolution_add_fusion = f32[1024,1440]{0,1:T(8,128)S(1)} fusion(bf16[1024,2880]{1,0:T(8,128)(2,1)} %bitcast.27, bf16[2880,1440]{0,1:T(8,128)(2,1)} %bitcast.26, f32[1440]{0:T(1024)S(1)} %reshape.271), kind=kOutput, calls=%fused_computation.5 | convolution fusion | flops 8494940160 | bytes 20096640 | tf_op jit(solution)/shard_map/dot_general | solution.py:54
  201.7 0.0 slice-done
  201.7 0.0 slice-done.1
  201.7 7.1 %convolution_convert_fusion = bf16[1024,2880]{0,1:T(8,128)(2,1)} fusion(bf16[1,720,2880]{2,1,0:T(8,128)(2,1)S(1)} %bitcast.29, f32[1024,1440]{0,1:T(8,128)S(1)} %convolution_add_fusion), kind=kOutput, calls=%fused_computation.3 | convolution fusion | flops 4257054720 | bytes 15943680 | tf_op jit(solution)/shard_map/dot_general | solution.py:59
  208.8 0.0 reduce-scatter.5.cloned.1.call-update
  208.8 73.0 %reduce-scatter.5.cloned.1.call-done = bf16[512,2880]{0,1:T(8,128)(2,1)} async-done(((bf16[1024,2880]{0,1:T(8,128)(2,1)}), bf16[512,2880]{0,1:T(8,128)(2,1)}) %reduce-scatter.5.cloned.1.call-update) | async-done | bytes 2949136 | tf_op jit(solution)/shard_map/reduce_scatter | solution.py:103
  281.8 4.6 %copy.28 = bf16[512,2880]{1,0:T(8,128)(2,1)} copy(bf16[512,2880]{0,1:T(8,128)(2,1)} %reduce-scatter.5.cloned.1.call-done) | data formatting | bytes 5898240 | tf_op jit(solution)/shard_map/reduce_scatter | solution.py:103
  286.3 0.0 copy-start.7
  286.3 6.5 %all-to-all-start.1 = ((bf16[16,32,2880]{2,1,0:T(8,128)(2,1)}), bf16[16,32,2880]{2,1,0:T(8,128)(2,1)S(1)}, u32[]{:S(2)}, u32[]{:S(2)}) async-start(bf16[16,32,2880]{2,1,0:T(8,128)(2,1)} %bitcast.22), calls=%async_computation.3 | async-start | bytes 6029312 | tf_op jit(solution)/shard_map/all_to_all | solution.py:109
  292.9 0.0 copy-done.7
  292.9 0.0 copy-done.10
  292.9 0.0 copy-done.11
  292.9 0.1 convolution_add_fusion.2
  293.2 0.1 copy.29
  293.2 0.1 div.32
  293.4 66.6 %all-to-all-done.1 = bf16[16,32,2880]{2,1,0:T(8,128)(2,1)S(1)} async-done(((bf16[16,32,2880]{2,1,0:T(8,128)(2,1)}), bf16[16,32,2880]{2,1,0:T(8,128)(2,1)S(1)}, u32[]{:S(2)}, u32[]{:S(2)}) %all-to-all-start.1) | async-done | bytes 2949152 | tf_op jit(solution)/shard_map/all_to_all | solution.py:109
  359.9 3.2 bitcast_convert_fusion
  363.1 4.5 %gather_fusion.1 = f32[128,2880]{1,0:T(8,128)S(1)} fusion(f32[512,2880]{1,0:T(8,128)} %bitcast_convert_fusion, s32[1024]{0:T(1024)S(1)} %pad_clamp_fusion), kind=kCustom, calls=%fused_computation.1.clone | custom fusion | bytes 2949632 | tf_op jit(solution)/shard_map/jit(_take)/gather | solution.py:46
  367.6 5.6 %gather_fusion = f32[128,2880]{1,0:T(8,128)} fusion(f32[512,2880]{1,0:T(8,128)} %bitcast_convert_fusion, s32[1024]{0:T(1024)S(1)} %pad_clamp_fusion.1), kind=kCustom, calls=%fused_computation.clone | custom fusion | bytes 2949632 | tf_op jit(solution)/shard_map/jit(_take)/gather | solution.py:45
  373.2 1.8 fusion.10
  375.0 0.0 copy-start.4
  375.0 0.4 reshape.270
  375.4 0.9 reduce_sum.67
  376.3 0.0 copy-done.4
  376.3 0.5 fusion.17
  376.8 0.0 copy-start.2
  376.8 0.8 fusion.19
  377.6 0.0 copy-done.2
  377.6 0.0 copy-done.1
  (19 shorter events, 0.2 us)
Async XLA Ops:
  7.2 1.0 copy-start
  7.2 9.7 %copy-start.9 = (s32[64,4]{0,1:T(4,128)S(1)}, s32[64,4]{0,1:T(4,128)}, u32[]{:S(2)}) copy-start(s32[64,4]{0,1:T(4,128)} %param.22) | copy-start | bytes 3076
  7.2 10.1 %copy-start.5 = (bf16[2880]{0:T(1024)(128)(2,1)S(1)}, bf16[2880]{0:T(1024)(128)(2,1)}, u32[]{:S(2)}) copy-start(bf16[2880]{0:T(1024)(128)(2,1)} %param.17) | copy-start | bytes 17284
  7.2 10.1 %copy-start.6 = (bf16[2880]{0:T(1024)(128)(2,1)S(1)}, bf16[2880]{0:T(1024)(128)(2,1)}, u32[]{:S(2)}) copy-start(bf16[2880]{0:T(1024)(128)(2,1)} %param.19) | copy-start | bytes 17284
  7.2 23.8 %copy-start.3 = (bf16[32,2880]{1,0:T(8,128)(2,1)S(1)}, bf16[32,2880]{1,0:T(8,128)(2,1)}, u32[]{:S(2)}) copy-start(bf16[32,2880]{1,0:T(8,128)(2,1)} %param.18) | copy-start | bytes 552964
  7.2 23.8 %reduce-scatter.3.cloned.1.call-start = ((), (), s32[]{:S(2)}) async-start(), calls=%async_computation.4 | async-start | bytes 565248 | tf_op jit(solution)/shard_map/reduce_scatter | solution.py:87
  16.9 171.1 %all-gather.3.cloned.1.call-start = ((), (), s32[]{:S(2)}) async-start(), calls=%async_computation.6 | async-start | bytes 9043968 | tf_op jit(solution)/shard_map/all_gather | solution.py:102
  111.5 0.7 copy-start.8
  111.5 90.1 %slice-start = ((s8[4239360]{0:T(1024)(128)(4,1)}), s8[45056]{0:T(1024)(128)(4,1)S(1)}, s32[]{:S(2)}) async-start(s8[4239360]{0:T(1024)(128)(4,1)} %bitcast.28), calls=%async_computation.7 | async-start | bytes 90112
  111.6 170.2 %reduce-scatter.5.cloned.1.call-start = ((), (), s32[]{:S(2)}) async-start(), calls=%async_computation.5 | async-start | bytes 8847360 | tf_op jit(solution)/shard_map/reduce_scatter | solution.py:103
  188.0 13.7 %slice-start.1 = ((s8[4239360]{0:T(1024)(128)(4,1)}), s8[4194304]{0:T(1024)(128)(4,1)S(1)}, s32[]{:S(2)}) async-start(s8[4239360]{0:T(1024)(128)(4,1)} %bitcast.28), calls=%async_computation.8 | async-start | bytes 8388608
  286.3 6.5 %copy-start.7 = (bf16[2880]{0:T(1024)(128)(2,1)S(1)}, bf16[2880]{0:T(1024)(128)(2,1)}, u32[]{:S(2)}) copy-start(bf16[2880]{0:T(1024)(128)(2,1)} %param.27) | copy-start | bytes 17284
  286.3 6.6 %copy-start.10 = (bf16[2880,8]{0,1:T(8,128)(2,1)S(1)}, bf16[2880,8]{0,1:T(8,128)(2,1)}, u32[]{:S(2)}) copy-start(bf16[2880,8]{0,1:T(8,128)(2,1)} %param.20) | copy-start | bytes 138244
  286.3 6.6 %copy-start.11 = (f32[8]{0:T(128)S(1)}, f32[8]{0:T(128)}, u32[]{:S(2)}) copy-start(f32[8]{0:T(128)} %param.21) | copy-start | bytes 100
  286.3 73.6 %all-to-all-start.1 = ((bf16[16,32,2880]{2,1,0:T(8,128)(2,1)}), bf16[16,32,2880]{2,1,0:T(8,128)(2,1)S(1)}, u32[]{:S(2)}, u32[]{:S(2)}) async-start(bf16[16,32,2880]{2,1,0:T(8,128)(2,1)} %bitcast.22), calls=%async_computation.3 | async-start | bytes 6029312 | tf_op jit(solution)/shard_map/all_to_all | solution.py:109
  373.2 4.4 %copy-start.1 = (bf16[64,2048]{1,0:T(8,128)(2,1)S(1)}, bf16[64,2048]{1,0:T(8,128)(2,1)}, u32[]{:S(2)}) copy-start(bf16[64,2048]{1,0:T(8,128)(2,1)} %param.15) | copy-start | bytes 786436
  375.0 1.4 copy-start.4
  376.8 0.8 copy-start.2
Sparse Core Ops, SparseCore 0:
  17.0 14.0 reduce-scatter.2
  111.7 76.2 all-gather.2
  208.9 72.7 reduce-scatter.4
where the time goes:
time: 385 us; the launch traced here: 384 us
  waiting for transfers between devices  229 us (59%)
  blocking collectives  73.3 us (19%)
  matrix products  30.1 us (8%)
  local copies, waits for them, and re-layouts  18.4 us (5%)
  between operations  14.1 us (4%)
  other arithmetic  13 us (3%)
  starting transfers between devices  6.81 us (2%)
    all_gather x1, waiting for transfers between devices, per_device(): lax.all_gather(incoming[None], 'tp', axis=0, tiled=True).reshape(-1, width)  75.7 us
    all_to_all x1, blocking collectives, per_device(): lax.all_to_all(outgoing, 'req', split_axis=0, concat_axis=0, tiled=True)  73.3 us
    reduce_scatter x1, waiting for transfers between devices, per_device(): lax.psum_scatter(expert_apply(gathered, gate_up_weight, gate_up_bias, dow...  73 us
    all_to_all x1, waiting for transfers between devices, per_device(): lax.all_to_all(sums.reshape(req_count, capacity, width).astype(jnp.bfloat...  66.6 us
    dot_general x1, matrix products, expert_apply(): projected = jnp.dot(rows, weight_mat, preferred_element_type=jnp.float32)  13.7 us
    reduce_scatter x1, waiting for transfers between devices, per_device(): lax.psum_scatter(jnp.dot(attn_ctx, o_weight, preferred_element_type=jnp.f...  13.3 us
    dot_general x1, matrix products, per_device(): jnp.dot(attn_ctx, o_weight, preferred_element_type=jnp.float32)  8.72 us
  transfers between devices with their start and end apart: 4, of which 4 were waited for; matrix products, arithmetic and copies ran while one was open for 0% of the time, Pallas kernels for 0%

commit v1 on v0

--- a/solution.py
+++ b/solution.py
@@ -59,6 +59,22 @@
     return jnp.dot(act, down_weight[0], preferred_element_type=jnp.float32)
 
 
+def dense_experts(normed, table, gate_up_weight, gate_up_bias, down_weight):
+    width = normed.shape[1]
+    expert = lax.axis_index("req") // 2
+    high = table.astype(jnp.bfloat16)
+    low = (table - high.astype(jnp.float32)).astype(jnp.bfloat16)
+    packed = jnp.concatenate([normed, high, low], axis=1)
+    gathered = lax.all_gather(packed, ("req", "tp"), axis=0, tiled=True)
+    count = table.shape[1]
+    pick = (jnp.arange(2 * count, dtype=jnp.int32) % count == expert).astype(jnp.float32)
+    share = jnp.sum(gathered[:, width:].astype(jnp.float32) * pick[None, :], axis=1, keepdims=True)
+    part = expert_apply(gathered[:, :width], gate_up_weight, gate_up_bias, down_weight) * share
+    return lax.psum_scatter(
+        part.astype(jnp.bfloat16), ("req", "tp"), scatter_dimension=0, tiled=True
+    ).astype(jnp.float32)
+
+
 def per_device(
     attn_ctx,
     o_weight,
@@ -95,6 +111,14 @@
     normed, weights, table = route_rows(
         state, own_routes, post_gain, router_weight, router_bias, experts
     )
+    bias_terms = jnp.dot(table, down_bias.astype(jnp.float32), precision=lax.Precision.HIGHEST)
+    if capacity == own_rows:
+        mixed = dense_experts(
+            normed, table, gate_up_weight, gate_up_bias, down_weight
+        )
+        hidden_state = (state.astype(jnp.float32) + mixed + bias_terms).astype(jnp.bfloat16)
+        normed_out = rms_norm(hidden_state.astype(jnp.float32), next_gain).astype(jnp.bfloat16)
+        return (hidden_state, normed_out)
     slots = slot_numbers(own_routes.reshape(1, own_rows * top_count), experts, capacity)
     targets = 2 * own_routes.reshape(-1) * capacity + slots.reshape(-1)
     outgoing = place_rows(normed, targets, capacity, req_count, top_count)
@@ -114,7 +138,6 @@
         tiled=True,
     ).astype(jnp.float32)
     mixed = weigh_parts(returned.reshape(-1, width), targets, capacity, weights, top_count)
-    bias_terms = jnp.dot(table, down_bias.astype(jnp.float32), precision=lax.Precision.HIGHEST)
     hidden_state = (state.astype(jnp.float32) + mixed + bias_terms).astype(jnp.bfloat16)
     normed_out = rms_norm(hidden_state.astype(jnp.float32), next_gain).astype(jnp.bfloat16)
     return (hidden_state, normed_out)

time: 385 us -> 282 us (0.73)
  the two profiles are of different devices: /device:TPU:13 before, /device:TPU:0 now
where the time goes in v1:
time: 282 us
  waiting for transfers between devices  228 us (81%)
  matrix products  33.4 us (12%)
  between operations  14 us (5%)
  other arithmetic  3.39 us (1%)
    reduce_scatter x1, waiting for transfers between devices, dense_experts(): lax.psum_scatter(part.astype(jnp.bfloat16), ('req', 'tp'), scatter_dimens...  144 us
    all_gather x1, waiting for transfers between devices, dense_experts(): gathered = lax.all_gather(packed, ('req', 'tp'), axis=0, tiled=True)  68.9 us
    reduce_scatter x1, waiting for transfers between devices, per_device(): lax.psum_scatter(jnp.dot(attn_ctx, o_weight, preferred_element_type=jnp.f...  15.6 us
    dot_general x1, matrix products, expert_apply(): projected = jnp.dot(rows, weight_mat, preferred_element_type=jnp.float32)  13.6 us
    dot_general x1, matrix products, expert_apply(): return jnp.dot(act, down_weight[0], preferred_element_type=jnp.float32)  9.55 us
    dot_general x1, matrix products, per_device(): jnp.dot(attn_ctx, o_weight, preferred_element_type=jnp.float32)  8.72 us
  transfers between devices with their start and end apart: 3, of which 3 were waited for; matrix products, arithmetic and copies ran while one was open for 0% of the time, Pallas kernels for 0%

profile of v1, /device:TPU:0, one launch (start us, length us, event | category | flops | bytes accessed | tf_op | source)
XLA Modules:
  0.0 281.7 jit_solution(16994743021834306350)
XLA Ops:
  7.2 0.0 copy-start
  7.2 0.0 copy-start.4
  7.2 0.0 copy-start.5
  7.2 0.0 copy-start.8
  7.2 0.0 copy-start.2
  7.2 0.0 copy-start.9
  7.2 0.0 copy-start.10
  7.2 0.0 copy-start.7
  7.3 0.0 reduce-scatter.3.cloned.1.call-start
  7.3 0.8 copy-done
  8.1 8.7 %convolution_convert_fusion = bf16[64,2880]{1,0:T(8,128)(2,1)} fusion(bf16[64,2048]{1,0:T(8,128)(2,1)S(1)} %copy-done, bf16[2048,2880]{0,1:T(8,128)(2,1)} %param.14), kind=kOutput, calls=%fused_computation.5 | convolution fusion | flops 755159040 | bytes 12427264 | tf_op jit(solution)/shard_map/dot_general | solution.py:104
  16.8 0.0 reduce-scatter.3.cloned.1.call-update
  16.9 0.0 all-gather.2.cloned.1.call-start
  16.9 0.0 copy-done.4
  17.0 0.0 copy-done.5
  17.0 0.0 copy-done.8
  17.0 0.1 constant_dynamic-slice_fusion
  17.1 15.6 %reduce-scatter.3.cloned.1.call-done = bf16[32,2880]{1,0:T(8,128)(2,1)} async-done(((bf16[64,2880]{1,0:T(8,128)(2,1)}), bf16[32,2880]{1,0:T(8,128)(2,1)}) %reduce-scatter.3.cloned.1.call-update) | async-done | bytes 184336 | tf_op jit(solution)/shard_map/reduce_scatter | solution.py:103
  32.7 0.0 copy-done.2
  32.7 1.1 fusion.19
  33.8 0.1 fusion.21
  33.9 0.0 copy-done.9
  33.9 0.0 copy-done.10
  33.9 0.1 convolution_add_fusion.1
  34.2 0.1 copy.19
  34.3 0.1 copy.20
  34.4 0.8 concatenate.3
  35.1 0.0 all-gather.2.cloned.1.call-update
  35.2 0.0 reduce-scatter.5.cloned.1.call-start
  35.2 0.0 copy-done.7
  35.2 0.1 reshape.64
  35.3 68.9 %all-gather.2.cloned.1.call-done = bf16[1024,2896]{1,0:T(8,128)(2,1)} async-done(((bf16[32,2896]{1,0:T(8,128)(2,1)}), bf16[1024,2896]{1,0:T(8,128)(2,1)}) %all-gather.2.cloned.1.call-update) | async-done | bytes 5931024 | tf_op jit(solution)/shard_map/all_gather | solution.py:68
  104.2 1.2 multiply_reduce_fusion
  105.4 13.6 %fusion.2 = f32[1024,1440]{0,1:T(8,128)S(1)} fusion(bf16[2880,1440]{0,1:T(8,128)(2,1)} %bitcast.11, bf16[1024,2896]{1,0:T(8,128)(2,1)} %all-gather.2.cloned.1.call-done, f32[1440]{0:T(1024)S(1)} %reshape.64), kind=kOutput, calls=%fused_computation.3 | convolution fusion | flops 8494940160 | bytes 20129408 | tf_op jit(solution)/shard_map/dot_general | solution.py:54
  119.0 9.5 %multiply_convert_fusion = bf16[1024,2880]{1,0:T(8,128)(2,1)} fusion(f32[1024]{0:T(1024)S(1)} %multiply_reduce_fusion, bf16[1,720,2880]{2,1,0:T(8,128)(2,1)} %param.23, f32[1024,1440]{0,1:T(8,128)S(1)} %fusion.2), kind=kOutput, calls=%fused_computation | convolution fusion | flops 4260003840 | bytes 15947776 | tf_op jit(solution)/shard_map/dot_general | solution.py:59
  128.6 0.0 copy-start.6
  128.6 0.0 copy-start.3
  128.6 0.0 reduce-scatter.5.cloned.1.call-update
  128.6 0.7 copy-done.6
  129.2 143.7 %reduce-scatter.5.cloned.1.call-done = bf16[32,2880]{1,0:T(8,128)(2,1)} async-done(((bf16[1024,2880]{1,0:T(8,128)(2,1)}), bf16[32,2880]{1,0:T(8,128)(2,1)}) %reduce-scatter.5.cloned.1.call-update) | async-done | bytes 184336 | tf_op jit(solution)/shard_map/reduce_scatter | solution.py:73
  272.9 0.0 copy-done.3
  273.0 1.4 fusion.16
  274.4 0.0 copy-start.1
  274.4 0.8 fusion.18
  275.2 0.0 copy-done.1
  (11 shorter events, 0.1 us)
Async XLA Ops:
  7.2 1.0 copy-start
  7.2 9.7 %copy-start.4 = (bf16[2880]{0:T(1024)(128)(2,1)S(1)}, bf16[2880]{0:T(1024)(128)(2,1)}, u32[]{:S(2)}) copy-start(bf16[2880]{0:T(1024)(128)(2,1)} %param.15) | copy-start | bytes 17284
  7.2 9.8 %copy-start.5 = (bf16[2880]{0:T(1024)(128)(2,1)S(1)}, bf16[2880]{0:T(1024)(128)(2,1)}, u32[]{:S(2)}) copy-start(bf16[2880]{0:T(1024)(128)(2,1)} %param.17) | copy-start | bytes 17284
  7.2 9.8 %copy-start.8 = (s32[64,4]{0,1:T(4,128)S(1)}, s32[64,4]{0,1:T(4,128)}, u32[]{:S(2)}) copy-start(s32[64,4]{0,1:T(4,128)} %param.20) | copy-start | bytes 3076
  7.2 25.4 %copy-start.2 = (bf16[32,2880]{1,0:T(8,128)(2,1)S(1)}, bf16[32,2880]{1,0:T(8,128)(2,1)}, u32[]{:S(2)}) copy-start(bf16[32,2880]{1,0:T(8,128)(2,1)} %param.16) | copy-start | bytes 552964
  7.2 26.7 %copy-start.9 = (bf16[2880,8]{0,1:T(8,128)(2,1)S(1)}, bf16[2880,8]{0,1:T(8,128)(2,1)}, u32[]{:S(2)}) copy-start(bf16[2880,8]{0,1:T(8,128)(2,1)} %param.18) | copy-start | bytes 138244
  7.2 26.7 %copy-start.10 = (f32[8]{0:T(128)S(1)}, f32[8]{0:T(128)}, u32[]{:S(2)}) copy-start(f32[8]{0:T(128)} %param.19) | copy-start | bytes 100
  7.2 28.0 %copy-start.7 = (bf16[1,2,720]{2,1,0:T(2,128)(2,1)S(1)}, bf16[1,2,720]{2,1,0:T(2,128)(2,1)}, u32[]{:S(2)}) copy-start(bf16[1,2,720]{2,1,0:T(2,128)(2,1)} %param.22) | copy-start | bytes 8644
  7.3 25.4 %reduce-scatter.3.cloned.1.call-start = ((), (), s32[]{:S(2)}) async-start(), calls=%async_computation.2 | async-start | bytes 565248 | tf_op jit(solution)/shard_map/reduce_scatter | solution.py:103
  16.9 87.3 %all-gather.2.cloned.1.call-start = ((), (), s32[]{:S(2)}) async-start(), calls=%async_computation.3 | async-start | bytes 6217728 | tf_op jit(solution)/shard_map/all_gather | solution.py:68
  35.2 237.8 %reduce-scatter.5.cloned.1.call-start = ((), (), s32[]{:S(2)}) async-start(), calls=%async_computation.4 | async-start | bytes 6217728 | tf_op jit(solution)/shard_map/reduce_scatter | solution.py:73
  128.6 0.7 copy-start.6
  128.6 144.4 %copy-start.3 = (bf16[8,2880]{1,0:T(8,128)(2,1)S(1)}, bf16[8,2880]{1,0:T(8,128)(2,1)}, u32[]{:S(2)}) copy-start(bf16[8,2880]{1,0:T(8,128)(2,1)} %param.24) | copy-start | bytes 138244
  274.4 0.8 copy-start.1
Sparse Core Ops, SparseCore 0:
  17.0 15.6 reduce-scatter.2
  36.1 68.0 all-gather.1
  128.7 144.2 reduce-scatter.4

commit v2 on v0

--- a/solution.py
+++ b/solution.py
@@ -1,6 +1,10 @@
+import functools
+
 import jax
 import jax.numpy as jnp
 from jax import lax
+from jax.experimental import pallas as pl
+from jax.experimental.pallas import tpu as pltpu
 from jax.sharding import PartitionSpec as P
 
 
@@ -57,6 +61,299 @@
     upper = jnp.clip(projected[:, local_width:], -7.0, 7.0)
     act = ((upper + 1.0) * gate * jax.nn.sigmoid(1.702 * gate)).astype(jnp.bfloat16)
     return jnp.dot(act, down_weight[0], preferred_element_type=jnp.float32)
+
+
+def top_bit(slot):
+    return slot.bit_length() - 1
+
+
+def by_hops(slots):
+    return sorted(slots, key=lambda slot: (bin(slot).count("1"), slot))
+
+
+def partner_of(axis, stride):
+    here = lax.axis_index(axis)
+    return here + stride * (1 - 2 * ((here // stride) % 2))
+
+
+def tree_copies(orders, rows, first_bit, last_bit):
+    half_rows = rows // 2
+    listed = {}
+    for bit in range(first_bit, last_bit):
+        for slot in range(1 << bit):
+            if orders[0][bit] == orders[1][bit]:
+                listed[(bit, slot, None)] = (slot * rows, rows)
+            else:
+                for half in range(2):
+                    listed[(bit, slot, half)] = (slot * rows + half * half_rows, half_rows)
+    return listed
+
+
+def exchange_kernel(
+    orders,
+    rows,
+    width,
+    experts,
+    x_ref,
+    gate_up_ref,
+    bias_ref,
+    down_ref,
+    out_ref,
+    gathered,
+    partial,
+    received,
+    gate_up,
+    down,
+    act,
+    weight_sems,
+    gather_send,
+    gather_recv,
+    reduce_send,
+    reduce_recv,
+):
+    bits = len(orders[0])
+    slots = 1 << bits
+    half_rows = rows // 2
+    hidden = down.shape[0]
+    chunk = slots // 4
+    span = chunk * rows
+    tail = width // 128 * 128
+    expert = lax.axis_index("req") // 2
+
+    loads = [
+        pltpu.make_async_copy(gate_up_ref, gate_up, weight_sems.at[0]),
+        pltpu.make_async_copy(down_ref, down, weight_sems.at[1]),
+    ]
+    for load in loads:
+        load.start()
+    barrier = pltpu.get_barrier_semaphore()
+    for axis, stride in orders[0]:
+        pl.semaphore_signal(
+            barrier,
+            inc=1,
+            device_id={axis: partner_of(axis, stride)},
+            device_id_type=pl.DeviceIdType.MESH,
+        )
+    gathered[0:rows, :] = x_ref[...]
+    pl.semaphore_wait(barrier, bits)
+
+    def remote(source, target, send_sem, recv_sem, link):
+        axis, stride = link
+        return pltpu.make_async_remote_copy(
+            src_ref=source,
+            dst_ref=target,
+            send_sem=send_sem,
+            recv_sem=recv_sem,
+            device_id={axis: partner_of(axis, stride)},
+            device_id_type=pl.DeviceIdType.MESH,
+        )
+
+    spread = {}
+    for number, (key, (row, length)) in enumerate(tree_copies(orders, rows, 0, bits).items()):
+        bit, slot, half = key
+        spread[key] = remote(
+            gathered.at[pl.ds(row, length), :],
+            gathered.at[pl.ds(row + (rows << bit), length), :],
+            gather_send.at[number],
+            gather_recv.at[number],
+            orders[half or 0][bit],
+        )
+
+    def forward(slot):
+        for bit in range(top_bit(slot) + 1, bits):
+            for half in (None, 0, 1):
+                if (bit, slot, half) in spread:
+                    spread[(bit, slot, half)].start()
+
+    def arrive(slot):
+        bit = top_bit(slot)
+        for half in (None, 0, 1):
+            key = (bit, slot - (1 << bit), half)
+            if key in spread:
+                spread[key].wait_recv()
+
+    def compute(first):
+        base = first * rows
+        block = pl.ds(base, span)
+        for start in range(0, hidden, 256):
+            size = min(256, hidden - start)
+            sides = []
+            for side in range(2):
+                sides.append(
+                    lax.dot_general(
+                        gathered[block, 0:width],
+                        gate_up[pl.ds(side * hidden + start, size), :],
+                        (((1,), (1,)), ((), ())),
+                        preferred_element_type=jnp.float32,
+                    )
+                    + bias_ref[side : side + 1, start : start + size]
+                )
+            gate = jnp.minimum(sides[0], 7.0)
+            upper = jnp.clip(sides[1], -7.0, 7.0)
+            act[:, start : start + size] = (
+                (upper + 1.0) * gate * jax.nn.sigmoid(1.702 * gate)
+            ).astype(jnp.bfloat16)
+        extra = gathered[block, tail:].astype(jnp.float32)
+        lane = lax.broadcasted_iota(jnp.int32, extra.shape, 1) - (width - tail)
+        mine = (lane == expert) | (lane == expert + experts)
+        share = jnp.sum(jnp.where(mine, extra, 0.0), axis=1, keepdims=True)
+        for start in range(0, width, 768):
+            size = min(768, width - start)
+            partial[block, start : start + size] = (
+                jnp.dot(
+                    act[...], down[:, start : start + size], preferred_element_type=jnp.float32
+                )
+                * share
+            ).astype(jnp.bfloat16)
+
+    fold = {}
+    number = 0
+    for first in (slots // 2, slots // 2 + chunk):
+        block = pl.ds(first * rows, span)
+        fold[("chunk", first)] = remote(
+            partial.at[block, :],
+            received.at[block, :],
+            reduce_send.at[number],
+            reduce_recv.at[number],
+            orders[0][bits - 1],
+        )
+        number += 1
+    for key, (row, length) in tree_copies(orders, rows, 0, bits - 1).items():
+        bit, slot, half = key
+        block = pl.ds(row + (rows << bit), length)
+        fold[(slot + (1 << bit), half)] = remote(
+            partial.at[block, :],
+            received.at[block, :],
+            reduce_send.at[number],
+            reduce_recv.at[number],
+            orders[half or 0][bit],
+        )
+        number += 1
+    landed = set()
+
+    def await_fold(slot, half):
+        if slot >= slots // 2:
+            key = ("chunk", slot // chunk * chunk)
+        else:
+            key = (slot, half) if (slot, half) in fold else (slot, None)
+        if key not in landed:
+            landed.add(key)
+            fold[key].wait_recv()
+
+    def reduce(slot):
+        for half in range(2):
+            first = slot * rows + half * half_rows
+            total = partial[first : first + half_rows, :].astype(jnp.float32)
+            for bit in reversed(range(top_bit(slot) + 1, bits)):
+                child = slot + (1 << bit)
+                await_fold(child, half)
+                begin = child * rows + half * half_rows
+                total = total + received[begin : begin + half_rows, :].astype(jnp.float32)
+            if slot == 0:
+                out_ref[half * half_rows : (half + 1) * half_rows, :] = total
+            else:
+                partial[first : first + half_rows, :] = total.astype(jnp.bfloat16)
+                if (slot, half) in fold:
+                    fold[(slot, half)].start()
+        if slot and (slot, None) in fold:
+            fold[(slot, None)].start()
+
+    forward(0)
+    for slot in by_hops(range(1, chunk)):
+        arrive(slot)
+        forward(slot)
+    for load in loads:
+        load.wait()
+    compute(0)
+    early = by_hops(range(chunk, 2 * chunk))
+    for slot in early[: chunk // 2]:
+        arrive(slot)
+        forward(slot)
+    for slot in range(2 * chunk, 3 * chunk):
+        arrive(slot)
+    compute(2 * chunk)
+    fold[("chunk", 2 * chunk)].start()
+    for slot in early[chunk // 2 :]:
+        arrive(slot)
+        forward(slot)
+    for slot in range(3 * chunk, 4 * chunk):
+        arrive(slot)
+    compute(3 * chunk)
+    fold[("chunk", 3 * chunk)].start()
+    compute(chunk)
+    for slot in reversed(early):
+        reduce(slot)
+    for slot in reversed(by_hops(range(0, chunk))):
+        reduce(slot)
+    for copy in spread.values():
+        copy.wait_send()
+    for copy in fold.values():
+        copy.wait_send()
+
+
+def tree_orders(req_count, tp_count):
+    strides = []
+    stride = 1
+    while stride < req_count:
+        strides.append(("req", stride))
+        stride *= 2
+    crosses = []
+    stride = 1
+    while stride < tp_count:
+        crosses.append(("tp", stride))
+        stride *= 2
+    return (
+        strides[2:] + strides[1:2] + crosses + strides[:1],
+        strides[2:] + crosses + strides[1:2] + strides[:1],
+    )
+
+
+def dense_experts(normed, table, gate_up_weight, gate_up_bias, down_weight):
+    rows, width = normed.shape
+    experts = table.shape[1]
+    orders = tree_orders(lax.axis_size("req"), lax.axis_size("tp"))
+    bits = len(orders[0])
+    hidden = down_weight.shape[1]
+    padded = (width + 2 * experts + 127) // 128 * 128
+    high = table.astype(jnp.bfloat16)
+    low = (table - high.astype(jnp.float32)).astype(jnp.bfloat16)
+    packed = jnp.concatenate(
+        [normed, high, low, jnp.zeros((rows, padded - width - 2 * experts), jnp.bfloat16)], axis=1
+    )
+    gate_up = jnp.transpose(gate_up_weight[0], (1, 2, 0)).reshape(2 * hidden, width)
+    bias = gate_up_bias[0].astype(jnp.float32)
+    total_rows = rows << bits
+    copies = len(tree_copies(orders, rows, 0, bits))
+    folds = 2 + len(tree_copies(orders, rows, 0, bits - 1))
+    vmem = pl.BlockSpec(memory_space=pltpu.VMEM)
+    anywhere = pl.BlockSpec(memory_space=pl.ANY)
+    return pl.pallas_call(
+        functools.partial(exchange_kernel, orders, rows, width, experts),
+        out_shape=jax.ShapeDtypeStruct((rows, width), jnp.float32),
+        in_specs=[vmem, anywhere, vmem, anywhere],
+        out_specs=vmem,
+        scratch_shapes=[
+            pltpu.VMEM((total_rows, padded), jnp.bfloat16),
+            pltpu.VMEM((total_rows, width), jnp.bfloat16),
+            pltpu.VMEM((total_rows, width), jnp.bfloat16),
+            pltpu.VMEM((2 * hidden, width), jnp.bfloat16),
+            pltpu.VMEM((hidden, width), jnp.bfloat16),
+            pltpu.VMEM((total_rows // 4, hidden), jnp.bfloat16),
+            pltpu.SemaphoreType.DMA((2,)),
+            pltpu.SemaphoreType.DMA((copies,)),
+            pltpu.SemaphoreType.DMA((copies,)),
+            pltpu.SemaphoreType.DMA((folds,)),
+            pltpu.SemaphoreType.DMA((folds,)),
+        ],
+        compiler_params=pltpu.CompilerParams(
+            collective_id=0, has_side_effects=True, vmem_limit_bytes=56 * 1024 * 1024
+        ),
+    )(packed, gate_up, bias, down_weight[0])
+
+
+def tree_fits(req_count, tp_count, rows):
+    count = req_count * tp_count
+    return count >= 16 and req_count >= 8 and tp_count >= 2 and count & (count - 1) == 0 and rows % 32 == 0
 
 
 def per_device(
@@ -95,6 +392,14 @@
     normed, weights, table = route_rows(
         state, own_routes, post_gain, router_weight, router_bias, experts
     )
+    bias_terms = jnp.dot(table, down_bias.astype(jnp.float32), precision=lax.Precision.HIGHEST)
+    if capacity == own_rows and tree_fits(req_count, tp_count, own_rows):
+        mixed = dense_experts(
+            normed, table, gate_up_weight, gate_up_bias, down_weight
+        )
+        hidden_state = (state.astype(jnp.float32) + mixed + bias_terms).astype(jnp.bfloat16)
+        normed_out = rms_norm(hidden_state.astype(jnp.float32), next_gain).astype(jnp.bfloat16)
+        return (hidden_state, normed_out)
     slots = slot_numbers(own_routes.reshape(1, own_rows * top_count), experts, capacity)
     targets = 2 * own_routes.reshape(-1) * capacity + slots.reshape(-1)
     outgoing = place_rows(normed, targets, capacity, req_count, top_count)
@@ -114,7 +419,6 @@
         tiled=True,
     ).astype(jnp.float32)
     mixed = weigh_parts(returned.reshape(-1, width), targets, capacity, weights, top_count)
-    bias_terms = jnp.dot(table, down_bias.astype(jnp.float32), precision=lax.Precision.HIGHEST)
     hidden_state = (state.astype(jnp.float32) + mixed + bias_terms).astype(jnp.bfloat16)
     normed_out = rms_norm(hidden_state.astype(jnp.float32), next_gain).astype(jnp.bfloat16)
     return (hidden_state, normed_out)

time: 385 us -> 132 us (0.34)
  the two profiles are of different devices: /device:TPU:13 before, /device:TPU:0 now
where the time goes in v2:
time: 132 us
  Pallas kernels  87.3 us (66%)
  waiting for transfers between devices  15 us (11%)
  between operations  14.3 us (11%)
  matrix products  10.3 us (8%)
  other arithmetic  2.74 us (2%)
  local copies, waits for them, and re-layouts  1.87 us (1%)
    pallas_call x1, Pallas kernels, dense_experts(): pl.pallas_call(functools.partial(exchange_kernel, orders, rows, width, ex...  87.3 us
    reduce_scatter x1, waiting for transfers between devices, per_device(): lax.psum_scatter(jnp.dot(attn_ctx, o_weight, preferred_element_type=jnp.f...  15 us
    dot_general x1, matrix products, per_device(): jnp.dot(attn_ctx, o_weight, preferred_element_type=jnp.float32)  8.72 us
  transfers between devices with their start and end apart: 1, of which 1 were waited for; matrix products, arithmetic and copies ran while one was open for 1% of the time, Pallas kernels for 0%

profile of v2, /device:TPU:0, one launch (start us, length us, event | category | flops | bytes accessed | tf_op | source)
XLA Modules:
  0.0 131.6 jit_solution(13702126701705645833)
XLA Ops:
  7.2 0.0 copy-start
  7.2 0.0 copy-start.4
  7.2 0.0 copy-start.5
  7.2 0.0 copy-start.6
  7.2 0.0 copy-start.8
  7.2 0.0 copy-start.7
  7.2 0.0 copy-start.2
  7.2 0.0 copy-start.9
  7.3 0.0 copy-start.10
  7.3 0.0 copy-start.3
  7.3 0.0 reduce-scatter.2.cloned.1.call-start
  7.3 0.8 copy-done
  8.1 8.7 %convolution_convert_fusion = bf16[64,2880]{1,0:T(8,128)(2,1)} fusion(bf16[64,2048]{1,0:T(8,128)(2,1)S(1)} %copy-done, bf16[2048,2880]{0,1:T(8,128)(2,1)} %param.14), kind=kOutput, calls=%fused_computation | convolution fusion | flops 755159040 | bytes 12427264 | tf_op jit(solution)/shard_map/dot_general | solution.py:385
  16.8 0.0 reduce-scatter.2.cloned.1.call-update
  16.9 0.0 copy-done.4
  16.9 0.0 copy-done.5
  16.9 0.0 copy-done.6
  16.9 0.0 copy-done.8
  17.0 0.1 constant_dynamic-slice_fusion
  17.0 0.0 copy-done.7
  17.0 0.6 bitcast_convert_fusion.bias_ref
  17.6 15.0 %reduce-scatter.2.cloned.1.call-done = bf16[32,2880]{1,0:T(8,128)(2,1)} async-done(((bf16[64,2880]{1,0:T(8,128)(2,1)}), bf16[32,2880]{1,0:T(8,128)(2,1)}) %reduce-scatter.2.cloned.1.call-update) | async-done | bytes 184336 | tf_op jit(solution)/shard_map/reduce_scatter | solution.py:384
  32.7 0.0 copy-done.2
  32.7 1.1 fusion.4
  33.8 0.1 fusion.6
  33.9 0.0 copy-done.9
  33.9 0.0 copy-done.10
  33.9 0.1 convolution_add_fusion.1
  34.2 0.1 copy.20
  34.3 0.1 copy.21
  34.4 0.8 concatenate.3.x_ref
  35.1 87.3 %shard_map.140 = f32[32,2880]{1,0:T(8,128)} custom-call(bf16[32,2944]{1,0:T(8,128)(2,1)} %concatenate.3.x_ref, bf16[1440,2880]{1,0:T(8,128)(2,1)} %bitcast.15, f32[2,720]{1,0:T(2,128)} %bitcast_convert_fusion.bias_ref, bf16[720,2880]{1,0:T(8,128)(2,1)} %bitcast.16), custom_call_target="tpu_custom_call" | custom-call | tf_op jit(solution)/shard_map/pallas_call | solution.py:330
  122.5 0.0 copy-done.3
  122.5 1.5 %fusion.1 = (f32[32]{0:T(128)S(1)}, bf16[32,2880]{1,0:T(8,128)(2,1)S(1)}) fusion(f32[32,8]{0,1:T(8,128)S(1)} %select_reduce_fusion, bf16[8,2880]{1,0:T(8,128)(2,1)S(1)} %copy-done.3, f32[32,2880]{1,0:T(8,128)} %shard_map.140, bf16[32,2880]{1,0:T(8,128)(2,1)S(1)} %get-tuple-element.3), kind=kOutput, calls=%fused_computation.9 | convolution fusion | flops 9492448 | bytes 784512 | tf_op jit(solution)/shard_map/dot_general | solution.py:395
  124.0 0.0 copy-start.1
  124.0 0.8 fusion.3
  124.8 0.0 copy-done.1
  (12 shorter events, 0.1 us)
Async XLA Ops:
  7.2 1.0 copy-start
  7.2 9.7 %copy-start.4 = (bf16[2880]{0:T(1024)(128)(2,1)S(1)}, bf16[2880]{0:T(1024)(128)(2,1)}, u32[]{:S(2)}) copy-start(bf16[2880]{0:T(1024)(128)(2,1)} %param.15) | copy-start | bytes 17284
  7.2 9.7 %copy-start.5 = (bf16[2880]{0:T(1024)(128)(2,1)S(1)}, bf16[2880]{0:T(1024)(128)(2,1)}, u32[]{:S(2)}) copy-start(bf16[2880]{0:T(1024)(128)(2,1)} %param.17) | copy-start | bytes 17284
  7.2 9.7 %copy-start.6 = (bf16[2880]{0:T(1024)(128)(2,1)S(1)}, bf16[2880]{0:T(1024)(128)(2,1)}, u32[]{:S(2)}) copy-start(bf16[2880]{0:T(1024)(128)(2,1)} %param.25) | copy-start | bytes 17284
  7.2 9.7 %copy-start.8 = (s32[64,4]{0,1:T(4,128)S(1)}, s32[64,4]{0,1:T(4,128)}, u32[]{:S(2)}) copy-start(s32[64,4]{0,1:T(4,128)} %param.20) | copy-start | bytes 3076
  7.2 9.8 %copy-start.7 = (bf16[1,2,720]{2,1,0:T(2,128)(2,1)S(1)}, bf16[1,2,720]{2,1,0:T(2,128)(2,1)}, u32[]{:S(2)}) copy-start(bf16[1,2,720]{2,1,0:T(2,128)(2,1)} %param.22) | copy-start | bytes 8644
  7.2 25.4 %copy-start.2 = (bf16[32,2880]{1,0:T(8,128)(2,1)S(1)}, bf16[32,2880]{1,0:T(8,128)(2,1)}, u32[]{:S(2)}) copy-start(bf16[32,2880]{1,0:T(8,128)(2,1)} %param.16) | copy-start | bytes 552964
  7.2 26.7 %copy-start.9 = (bf16[2880,8]{0,1:T(8,128)(2,1)S(1)}, bf16[2880,8]{0,1:T(8,128)(2,1)}, u32[]{:S(2)}) copy-start(bf16[2880,8]{0,1:T(8,128)(2,1)} %param.18) | copy-start | bytes 138244
  7.3 26.7 %copy-start.10 = (f32[8]{0:T(128)S(1)}, f32[8]{0:T(128)}, u32[]{:S(2)}) copy-start(f32[8]{0:T(128)} %param.19) | copy-start | bytes 100
  7.3 115.2 %copy-start.3 = (bf16[8,2880]{1,0:T(8,128)(2,1)S(1)}, bf16[8,2880]{1,0:T(8,128)(2,1)}, u32[]{:S(2)}) copy-start(bf16[8,2880]{1,0:T(8,128)(2,1)} %param.24) | copy-start | bytes 138244
  7.3 25.4 %reduce-scatter.2.cloned.1.call-start = ((), (), s32[]{:S(2)}) async-start(), calls=%async_computation.1 | async-start | bytes 565248 | tf_op jit(solution)/shard_map/reduce_scatter | solution.py:384
  124.0 0.8 copy-start.1
Sparse Core Ops, SparseCore 0:
  17.0 15.6 reduce-scatter.1

commit v3 on v2

--- a/solution.py
+++ b/solution.py
@@ -381,12 +381,14 @@
     capacity = min(own_rows, max(2, 2 * top_count * own_rows // experts))
     own_start = lax.axis_index("tp") * own_rows
     bias_vec = o_bias.astype(jnp.float32)
-    summed = lax.psum_scatter(
-        jnp.dot(attn_ctx, o_weight, preferred_element_type=jnp.float32).astype(jnp.bfloat16),
-        "tp",
-        scatter_dimension=0,
-        tiled=True,
-    ).astype(jnp.float32)
+    proj = jnp.dot(attn_ctx, o_weight, preferred_element_type=jnp.float32).astype(jnp.bfloat16)
+    if tp_count == 2:
+        theirs = lax.dynamic_slice_in_dim(proj, own_rows - own_start, own_rows, 0)
+        mine = lax.dynamic_slice_in_dim(proj, own_start, own_rows, 0)
+        arrived = lax.ppermute(theirs, "tp", [(0, 1), (1, 0)])
+        summed = mine.astype(jnp.float32) + arrived.astype(jnp.float32)
+    else:
+        summed = lax.psum_scatter(proj, "tp", scatter_dimension=0, tiled=True).astype(jnp.float32)
     state = (residual.astype(jnp.float32) + summed + bias_vec).astype(jnp.bfloat16)
     own_routes = lax.dynamic_slice_in_dim(routes, own_start, own_rows, 0)
     normed, weights, table = route_rows(

time: 132 us -> 109 us (0.83)
  between operations: 14.3 us -> 0.85 us
  waiting for transfers between devices: 15 us -> 3.99 us
  starting transfers between devices: 0.04 us -> 3 us
    reduce_scatter x1 -> x0, waiting for transfers between devices: 15 us -> none  [per_device(): lax.psum_scatter(jnp.dot(attn_ctx, o_weight, preferred_element_type=jnp.f...]
    ppermute x0 -> x1, waiting for transfers between devices: none -> 3.99 us  [per_device(): arrived = lax.ppermute(theirs, 'tp', [(0, 1), (1, 0)])]
    ppermute x0 -> x1, starting transfers between devices: none -> 3 us  [per_device(): arrived = lax.ppermute(theirs, 'tp', [(0, 1), (1, 0)])]
where the time goes in v3:
time: 109 us; the launch traced here: 108 us
  Pallas kernels  87.2 us (80%)
  matrix products  9.61 us (9%)
  waiting for transfers between devices  3.99 us (4%)
  starting transfers between devices  3 us (3%)
  local copies, waits for them, and re-layouts  1.95 us (2%)
  other arithmetic  1.84 us (2%)
    pallas_call x1, Pallas kernels, dense_experts(): pl.pallas_call(functools.partial(exchange_kernel, orders, rows, width, ex...  87.2 us
    dot_general x1, matrix products, per_device(): jnp.dot(attn_ctx, o_weight, preferred_element_type=jnp.float32)  7.99 us
    ppermute x1, waiting for transfers between devices, per_device(): arrived = lax.ppermute(theirs, 'tp', [(0, 1), (1, 0)])  3.99 us
    ppermute x1, starting transfers between devices, per_device(): arrived = lax.ppermute(theirs, 'tp', [(0, 1), (1, 0)])  3 us
  transfers between devices with their start and end apart: 1, of which 1 were waited for; matrix products, arithmetic and copies ran while one was open for 1% of the time, Pallas kernels for 0%

profile of v3, /device:TPU:0, one launch (start us, length us, event | category | flops | bytes accessed | tf_op | source)
XLA Modules:
  0.0 108.5 jit_solution(11885345723407761997)
XLA Ops:
  0.6 0.0 copy-start
  0.6 0.0 copy-start.4
  0.7 0.0 copy-start.5
  0.7 0.0 copy-start.6
  0.7 0.0 copy-start.8
  0.7 0.0 copy-start.7
  0.7 0.0 copy-start.2
  0.7 0.0 copy-start.9
  0.7 0.0 copy-start.10
  0.7 0.9 copy-done
  1.6 0.0 copy-start.3
  1.6 8.0 %convolution_convert_fusion = bf16[64,2880]{1,0:T(8,128)(2,1)S(1)} fusion(bf16[64,2048]{1,0:T(8,128)(2,1)S(1)} %copy-done, bf16[2048,2880]{0,1:T(8,128)(2,1)} %param.14), kind=kOutput, calls=%fused_computation | convolution fusion | flops 755159040 | bytes 12427264 | tf_op jit(solution)/shard_map/dot_general | solution.py:384
  9.6 3.0 %collective-permute-start = (bf16[32,2880]{1,0:T(8,128)(2,1)S(1)}, bf16[32,2880]{1,0:T(8,128)(2,1)S(1)}, u32[]{:S(2)}, u32[]{:S(2)}) collective-permute-start(bf16[32,2880]{1,0:T(8,128)(2,1)S(1)} %constant_dynamic-slice_fusion.1), channel_id=1, source_target_pairs={{0,1},{1,0},{2,3},{3,2},{4,5},{5,4},{6,7},{7,6},{8,9},{9,8},{10,11... | collective-permute-start | bytes 552968 | tf_op jit(solution)/shard_map/ppermute | solution.py:388
  12.6 0.0 copy-done.4
  12.6 0.0 copy-done.5
  12.7 0.0 copy-done.6
  12.7 0.0 copy-done.8
  12.7 0.1 constant_dynamic-slice_fusion
  12.8 0.0 copy-done.7
  12.8 0.6 bitcast_convert_fusion.bias_ref
  13.4 4.0 %collective-permute-done = bf16[32,2880]{1,0:T(8,128)(2,1)S(1)} collective-permute-done((bf16[32,2880]{1,0:T(8,128)(2,1)S(1)}, bf16[32,2880]{1,0:T(8,128)(2,1)S(1)}, u32[]{:S(2)}, u32[]{:S(2)}) %collective-permute-start) | collective-permute-done | bytes 184352 | tf_op jit(solution)/shard_map/ppermute | solution.py:388
  17.4 0.0 copy-done.2
  17.4 0.2 fusion.4
  17.6 0.1 fusion.6
  17.7 0.0 copy-done.9
  17.7 0.0 copy-done.10
  17.7 0.1 convolution_add_fusion.1
  18.0 0.1 copy.20
  18.1 0.1 copy.21
  18.2 0.8 concatenate.3.x_ref
  18.9 87.2 %shard_map.140 = f32[32,2880]{1,0:T(8,128)} custom-call(bf16[32,2944]{1,0:T(8,128)(2,1)} %concatenate.3.x_ref, bf16[1440,2880]{1,0:T(8,128)(2,1)} %bitcast.15, f32[2,720]{1,0:T(2,128)} %bitcast_convert_fusion.bias_ref, bf16[720,2880]{1,0:T(8,128)(2,1)} %bitcast.16), custom_call_target="tpu_custom_call" | custom-call | tf_op jit(solution)/shard_map/pallas_call | solution.py:330
  106.2 0.0 copy-done.3
  106.2 1.5 %fusion.1 = (f32[32]{0:T(128)S(1)}, bf16[32,2880]{1,0:T(8,128)(2,1)S(1)}) fusion(f32[32,8]{0,1:T(8,128)S(1)} %select_reduce_fusion, bf16[8,2880]{1,0:T(8,128)(2,1)S(1)} %copy-done.3, f32[32,2880]{1,0:T(8,128)} %shard_map.140, bf16[32,2880]{1,0:T(8,128)(2,1)S(1)} %get-tuple-element.3), kind=kOutput, calls=%fused_computation.9 | convolution fusion | flops 9492448 | bytes 784512 | tf_op jit(solution)/shard_map/dot_general | solution.py:397
  107.7 0.0 copy-start.1
  107.7 0.8 fusion.3
  108.5 0.0 copy-done.1
  (13 shorter events, 0.1 us)
Async XLA Ops:
  0.6 1.0 copy-start
  0.6 12.0 %copy-start.4 = (bf16[2880]{0:T(1024)(128)(2,1)S(1)}, bf16[2880]{0:T(1024)(128)(2,1)}, u32[]{:S(2)}) copy-start(bf16[2880]{0:T(1024)(128)(2,1)} %param.15) | copy-start | bytes 17284
  0.7 12.0 %copy-start.5 = (bf16[2880]{0:T(1024)(128)(2,1)S(1)}, bf16[2880]{0:T(1024)(128)(2,1)}, u32[]{:S(2)}) copy-start(bf16[2880]{0:T(1024)(128)(2,1)} %param.17) | copy-start | bytes 17284
  0.7 12.0 %copy-start.6 = (bf16[2880]{0:T(1024)(128)(2,1)S(1)}, bf16[2880]{0:T(1024)(128)(2,1)}, u32[]{:S(2)}) copy-start(bf16[2880]{0:T(1024)(128)(2,1)} %param.25) | copy-start | bytes 17284
  0.7 12.0 %copy-start.8 = (s32[64,4]{0,1:T(4,128)S(1)}, s32[64,4]{0,1:T(4,128)}, u32[]{:S(2)}) copy-start(s32[64,4]{0,1:T(4,128)} %param.20) | copy-start | bytes 3076
  0.7 12.1 %copy-start.7 = (bf16[1,2,720]{2,1,0:T(2,128)(2,1)S(1)}, bf16[1,2,720]{2,1,0:T(2,128)(2,1)}, u32[]{:S(2)}) copy-start(bf16[1,2,720]{2,1,0:T(2,128)(2,1)} %param.22) | copy-start | bytes 8644
  0.7 16.7 %copy-start.2 = (bf16[32,2880]{1,0:T(8,128)(2,1)S(1)}, bf16[32,2880]{1,0:T(8,128)(2,1)}, u32[]{:S(2)}) copy-start(bf16[32,2880]{1,0:T(8,128)(2,1)} %param.16) | copy-start | bytes 552964
  0.7 17.0 %copy-start.9 = (bf16[2880,8]{0,1:T(8,128)(2,1)S(1)}, bf16[2880,8]{0,1:T(8,128)(2,1)}, u32[]{:S(2)}) copy-start(bf16[2880,8]{0,1:T(8,128)(2,1)} %param.18) | copy-start | bytes 138244
  0.7 17.0 %copy-start.10 = (f32[8]{0:T(128)S(1)}, f32[8]{0:T(128)}, u32[]{:S(2)}) copy-start(f32[8]{0:T(128)} %param.19) | copy-start | bytes 100
  1.6 104.6 %copy-start.3 = (bf16[8,2880]{1,0:T(8,128)(2,1)S(1)}, bf16[8,2880]{1,0:T(8,128)(2,1)}, u32[]{:S(2)}) copy-start(bf16[8,2880]{1,0:T(8,128)(2,1)} %param.24) | copy-start | bytes 138244
  9.6 7.7 %collective-permute-start = (bf16[32,2880]{1,0:T(8,128)(2,1)S(1)}, bf16[32,2880]{1,0:T(8,128)(2,1)S(1)}, u32[]{:S(2)}, u32[]{:S(2)}) collective-permute-start(bf16[32,2880]{1,0:T(8,128)(2,1)S(1)} %constant_dynamic-slice_fusion.1), channel_id=1, source_target_pairs={{0,1},{1,0},{2,3},{3,2},{4,5},{5,4},{6,7},{7,6},{8,9},{9,8},{10,11... | collective-permute-start | bytes 552968 | tf_op jit(solution)/shard_map/ppermute | solution.py:388
  107.7 0.8 copy-start.1
